TPU v7x, 256 devices: a whole 4x4x8 slice. The times are simulated.
256 devices in a mesh: half: 2 (over core), cls: 2 (over y_lo), img: 64 (over y_hi, z, x).
Axes of the slice: x: 4, y: 4 (y_hi: 2, y_lo: 2; y = y_hi * 2 + y_lo), z: 8, core: 2. Of those that a mesh axis runs over, the one named last changes fastest.
Arguments:
- images: bfloat16 [2, 32768, 2, 8320], P('half', ('cls', 'img')), may hold values from -8 to 8
- projections: bfloat16 [2, 8, 8, 2, 8320], P('half', 'cls', None, None, 'img'), may hold values from -8 to 8
- ctf_table: float32 [2, 32, 8320], P('half'), may hold values from -1 to 1
- ctf_group: int32 [2, 32768], P('half', ('cls', 'img')), may hold values from 0 to 31
- orient_ids: int32 [2, 32768, 4], P('half', ('cls', 'img')), may hold values from 0 to 7
- trans_ids: int32 [2, 8], P('half'), may hold values from 0 to 24
- inv_sigma: float32 [2, 8320], P('half'), may hold values from 0.5 to 2
- counts: int32 [2, 128], P('half', ('cls', 'img')), may hold values from 1 to 256, 20480 in all within a row
Outputs:
- posterior: bfloat16 [2, 32768, 512], P('half', ('cls', 'img'))
- slab: float32 [2, 8, 8, 2, 8320], P('half', 'cls', None, None, 'img')
- fsc_map: float32 [2, 8, 8, 8320], P('half', 'cls', None, 'img')
Inputs may be any that keep to these rules, and one draw needn't show every extreme that they name: counts[h, s] is the number of live particles of shard s, held in its first slots; each half-set's counts sum to 20480, and the largest is 256.
All inputs are finite; a program needn't handle non-finite values.
Results may differ from a plain program's by a relative error of at most 0.013.
The roundings to bfloat16 on the way count: a program that leaves them out, or rounds other values in their place, can miss the bound.
Values may be sent and summed in bfloat16 or wider, within the bound.
No kernel may reach another device: no remote copies, remote signals or barrier semaphores. Data moves between devices by JAX's collectives and lax.ppermute only.
A program may use at most 192 MiB of HBM per device.

v0:
```python
import math
import jax
import jax.numpy as jnp
from jax import lax
from jax.sharding import PartitionSpec as P

K = 8
BOX = 128
O = 8
TR = 8
TGRID = 5


def swapped(value, axis, bit):
    return lax.ppermute(value, axis, [(i, i ^ 1 << bit) for i in range(lax.axis_size(axis))])


def phases(trans_list, count):
    half_width = BOX // 2 + 1
    freq_index = jnp.arange(count, dtype=jnp.int32)
    row_index = freq_index // half_width
    col_index = freq_index % half_width
    wave_x = (row_index - BOX * (row_index >= BOX // 2).astype(jnp.int32)).astype(jnp.float32)
    wave_y = col_index.astype(jnp.float32)
    shift_x = (trans_list % TGRID - TGRID // 2).astype(jnp.float32)
    shift_y = (trans_list // TGRID - TGRID // 2).astype(jnp.float32)
    angle = (
        2.0
        * math.pi
        / BOX
        * (shift_x[:, None] * wave_x[None, :] + shift_y[:, None] * wave_y[None, :])
    )
    return (jnp.cos(angle), jnp.sin(angle))


def shift_sections(sections, inverse, cosine, sine):
    real_part = sections[:, :, 0, :].astype(jnp.float32) * inverse
    imag_part = sections[:, :, 1, :].astype(jnp.float32) * inverse
    shifted_re = real_part[:, :, None, :] * cosine - imag_part[:, :, None, :] * sine
    shifted_im = real_part[:, :, None, :] * sine + imag_part[:, :, None, :] * cosine
    return jnp.stack([shifted_re, shifted_im], axis=3).astype(jnp.bfloat16)


def section_power(sections):
    real_part = sections[:, :, 0, :].astype(jnp.float32)
    imag_part = sections[:, :, 1, :].astype(jnp.float32)
    total = real_part * real_part + imag_part * imag_part
    return total.reshape(-1, total.shape[-1])


def contract_last(left, right):
    return lax.dot_general(
        left, right, (((1,), (1,)), ((), ())), preferred_element_type=jnp.float32
    )


def contract_high(left, right):
    return lax.dot_general(
        left,
        right,
        (((1,), (1,)), ((), ())),
        precision=lax.Precision.HIGHEST,
        preferred_element_type=jnp.float32,
    )


def on_device(images, projections, ctf_table, ctf_group, orient_ids, trans_ids, inv_sigma, counts):
    num_rows = images.shape[1]
    freqs = images.shape[3]
    groups = ctf_table.shape[1]
    inverse = inv_sigma[0]
    table = ctf_table[0]
    onehot = (ctf_group[0][:, None] == jnp.arange(groups, dtype=jnp.int32)[None, :]).astype(
        jnp.float32
    )
    ctf_rows = jnp.dot(
        onehot, table, precision=lax.Precision.HIGHEST, preferred_element_type=jnp.float32
    )
    weighted = (ctf_rows[:, None, :] * images[0].astype(jnp.float32)).astype(jnp.bfloat16)
    flat_images = weighted.reshape(num_rows, 2 * freqs)
    ctf_power = table * table * inverse
    translations = trans_ids[0]
    cosine, sine = phases(translations, freqs)
    full_sections = lax.all_gather(projections[0], "img", axis=3, tiled=True)
    piece = lax.all_gather(full_sections, "cls", axis=0, tiled=True)
    number = piece.shape[0]
    shifted = shift_sections(piece, inverse, cosine, sine).reshape(number * O * TR, 2 * freqs)
    cross_terms = contract_last(flat_images, shifted)
    norm_rows = jnp.dot(
        onehot,
        contract_high(ctf_power, section_power(piece)),
        precision=lax.Precision.HIGHEST,
        preferred_element_type=jnp.float32,
    )
    block = (
        cross_terms.reshape(num_rows, number, O, TR)
        - 0.5 * norm_rows.reshape(num_rows, number, O)[:, :, :, None]
    )
    allowed = jnp.any(
        orient_ids[0][:, :, None] == jnp.arange(O, dtype=jnp.int32)[None, None, :], axis=1
    )
    mask = jnp.broadcast_to(allowed[:, None, :, None], block.shape)
    top = jnp.max(jnp.where(mask, block, -jnp.inf), axis=(1, 2, 3), keepdims=True)
    expo = jnp.exp(jnp.where(mask, block - top, -jnp.inf))
    total = jnp.sum(expo, axis=(1, 2, 3), keepdims=True)
    live = (jnp.arange(num_rows, dtype=jnp.int32) < counts[0, 0]).astype(jnp.float32)
    weights = (expo / total * live[:, None, None, None]).astype(jnp.bfloat16)
    per_class = jnp.moveaxis(weights, 1, 0).reshape(K, num_rows, O * TR)

    def back_class(class_weights):
        summed = lax.dot_general(
            class_weights, flat_images, (((0,), (0,)), ((), ())), preferred_element_type=jnp.float32
        )
        summed = summed.reshape(O, TR, 2, freqs)
        slab_re = jnp.sum(summed[:, :, 0] * cosine + summed[:, :, 1] * sine, axis=1)
        slab_im = jnp.sum(summed[:, :, 1] * cosine - summed[:, :, 0] * sine, axis=1)
        return jnp.stack([slab_re, slab_im], axis=1)

    terms = lax.map(back_class, per_class)
    spread = lax.psum_scatter(terms, "img", scatter_dimension=3, tiled=True)
    own_slab = lax.psum_scatter(
        spread.astype(jnp.bfloat16), "cls", scatter_dimension=0, tiled=True
    ).astype(jnp.float32)
    partner = swapped(own_slab.astype(jnp.bfloat16), "half", 0).astype(own_slab.dtype)
    product = own_slab[:, :, 0] * partner[:, :, 0] + own_slab[:, :, 1] * partner[:, :, 1]
    return (weights.reshape(num_rows, K * O * TR)[None], own_slab[None], product[None])


def solution(mesh):
    return jax.shard_map(
        on_device,
        mesh=mesh,
        in_specs=(
            P("half", ("cls", "img"), None, None),
            P("half", "cls", None, None, "img"),
            P("half", None, None),
            P("half", ("cls", "img")),
            P("half", ("cls", "img"), None),
            P("half", None),
            P("half", None),
            P("half", ("cls", "img")),
        ),
        out_specs=(
            P("half", ("cls", "img"), None),
            P("half", "cls", None, None, "img"),
            P("half", "cls", None, "img"),
        ),
        check_vma=False,
    )
```

profile of v0, /device:TPU:1, one launch (start us, length us, event | category | flops | bytes accessed | tf_op | source)
XLA Modules:
  0.0 803.9 jit_solution(14484269285956258049)
XLA Ops:
  7.2 1.8 copy.37
  11.2 7.0 fusion.25
  18.2 9.1 %copy.56 = f32[256,8320]{0,1:T(8,128)} copy(f32[256,8320]{1,0:T(8,128)} %fusion.25) | data formatting | bytes 17039360
  27.3 24.2 %copy.41 = f32[1,256,2,8320]{1,3,2,0:T(8,128)} copy(bf16[1,256,2,8320]{3,2,1,0:T(2,128)(2,1)} %param.10) | data formatting | bytes 25559040 | tf_op jit(solution)/shard_map/convert_element_type | solution.py:79
  51.6 25.4 %fusion.14 = bf16[256,16640]{0,1:T(8,128)(2,1)} fusion(f32[1,256,2,8320]{1,3,2,0:T(8,128)} %copy.41, f32[256,8320]{0,1:T(8,128)} %copy.56), kind=kLoop, calls=%fused_computation.20 | loop fusion | flops 8519680 | bytes 34078720 | tf_op jit(solution)/shard_map/convert_element_type | solution.py:79
  78.2 11.5 %fusion.16 = bf16[256,2,8320,1,1]{2,1,0,4,3:T(2,128)(2,1)} fusion(f32[256,8320]{1,0:T(8,128)} %fusion.25, bf16[1,256,2,8320]{3,2,1,0:T(2,128)(2,1)} %param.10), kind=kLoop, calls=%fused_computation.25 | loop fusion | flops 12779520 | bytes 25559040 | tf_op jit(solution)/shard_map/convert_element_type | solution.py:79
  89.8 125.0 %all-gather.5.cloned.1.call-done = bf16[1,4,8,2,8320]{2,1,3,0,4:T(4,128)(2,1)} async-done(((bf16[1,4,8,2,130]{2,1,3,0,4:T(4,128)(2,1)}), bf16[1,4,8,2,8320]{2,1,3,0,4:T(4,128)(2,1)}) %all-gather.5.cloned.1.call-update) | async-done | bytes 1064976 | tf_op jit(solution)/shard_map/all_gather | solution.py:84
  214.8 19.8 %copy.38 = bf16[1,4,8,2,8320]{4,2,3,0,1:T(8,128)(2,1)} copy(bf16[1,4,8,2,8320]{2,1,3,0,4:T(4,128)(2,1)} %all-gather.5.cloned.1.call-done) | data formatting | bytes 2129920 | tf_op jit(solution)/shard_map/all_gather | solution.py:84
  235.7 34.9 %all-gather.7.cloned.1.call-done = bf16[1,8,8,2,8320]{4,2,3,0,1:T(8,128)(2,1)} async-done(((bf16[1,4,8,2,8320]{4,2,3,0,1:T(8,128)(2,1)}), bf16[1,8,8,2,8320]{4,2,3,0,1:T(8,128)(2,1)}) %all-gather.7.cloned.1.call-update) | async-done | bytes 2129936 | tf_op jit(solution)/shard_map/all_gather | solution.py:85
  270.6 2.0 fusion.18
  272.9 2.2 fusion.21
  275.4 7.4 subtract_convert_fusion
  282.8 10.9 %select_reduce_fusion = (f32[256]{0:T(256)S(1)}, f32[256,8,8,8,1]{0,3,4,2,1:T(8,128)S(1)}) fusion(f32[256,8,8]{0,2,1:T(8,128)S(1)} %bitcast.140, pred[256,8]{0,1:T(8,128)(4,1)S(1)} %fusion.54, bf16[8,8,8,1,8320]{4,2,3,1,0:T(8,128)(2,1)} %get-tuple-element.131, bf16[8,8,8,1,8320]{4,2,3,1,0:T(8,128)(2,1)} %get-tuple-element.130, ...), kind=kOutput, calls=%fused_computation.54 | convolution fusion | flops 4396548096 | bytes 26151936 | tf_op jit(solution)/shard_map/dot_general | solution.py:52
  294.0 83.4 %while.12 = (s32[]{:T(128)}, f32[8,8,2,8320]{3,1,2,0:T(8,128)}, bf16[8,256,64]{1,2,0:T(8,128)(2,1)S(1)}, bf16[256,16640]{0,1:T(8,128)(2,1)}, f32[8320]{0:T(1024)...) while((s32[]{:T(128)}, f32[8,8,2,8320]{3,1,2,0:T(8,128)}, ...), condition=%wide.region_6.7_spmd.clone.clone, body=%wide.region_3.6_spmd.clone.clone.sunk | while | flops 549785600 | bytes 21931680 | solution.py:119
  295.1 6.1 fusion.68
  305.5 6.1 fusion.68
  315.9 6.1 fusion.68
  326.3 6.1 fusion.68
  336.7 6.1 fusion.68
  347.1 6.1 fusion.68
  357.6 6.1 fusion.68
  368.0 6.1 fusion.68
  377.4 356.2 %all-reduce.2 = bf16[8,8,2,8320]{3,1,2,0:T(8,128)(2,1)S(1)} all-reduce(f32[8,8,2,8320]{3,1,2,0:T(8,128)} %get-tuple-element.35), channel_id=4, replica_groups=mesh['half'=2,'cls'=2,'img'=64] {'img'}, use_global_device_ids=true, to_apply=%region_7.8.clone | all-reduce | flops 1064960 | bytes 6389760
  735.3 58.8 %reduce-scatter.3.cloned.1.call-done = bf16[4,8,2,130]{3,1,2,0:T(8,128)(2,1)} async-done(((bf16[8,8,2,130]{3,1,2,0:T(8,128)(2,1)}), bf16[4,8,2,130]{3,1,2,0:T(8,128)(2,1)}) %reduce-scatter.3.cloned.1.call-update) | async-done | bytes 16656 | tf_op jit(solution)/shard_map/reduce_scatter | solution.py:121
  (84 shorter events, 43.3 us)
Async XLA Ops:
  7.2 207.6 %all-gather.5.cloned.1.call-start = ((), (), s32[]{:S(2)}) async-start(), calls=%async_computation.2 | async-start | bytes 17305600 | tf_op jit(solution)/shard_map/all_gather | solution.py:84
  9.1 261.5 %all-gather.7.cloned.1.call-start = ((), (), s32[]{:S(2)}) async-start(), calls=%async_computation.3 | async-start | bytes 3194880 | tf_op jit(solution)/shard_map/all_gather | solution.py:85
  27.3 24.2 %copy-start.2 = (f32[1,8320]{1,0:T(1,128)S(1)}, f32[1,8320]{1,0:T(1,128)}, u32[]{:S(2)}) copy-start(f32[1,8320]{1,0:T(1,128)} %param.16) | copy-start | bytes 99844
  51.6 25.4 %copy-start.4 = (u32[256]{0:T(256)S(1)}, u32[256]{0:T(256)}, u32[]{:S(2)}) copy-start(u32[256]{0:T(256)} %constant.79) | copy-start | bytes 3076
  234.6 38.1 %copy-start.1 = (f32[1,32,8320]{2,1,0:T(8,128)S(1)}, f32[1,32,8320]{2,1,0:T(8,128)}, u32[]{:S(2)}) copy-start(f32[1,32,8320]{2,1,0:T(8,128)} %param.12) | copy-start | bytes 3194884
  234.6 559.5 %reduce-scatter.3.cloned.1.call-start = ((), (), s32[]{:S(2)}) async-start(), calls=%async_computation.1 | async-start | bytes 98304 | tf_op jit(solution)/shard_map/reduce_scatter | solution.py:121
  270.6 2.2 copy-start
  270.6 4.5 copy-start.3
  794.1 2.6 collective-permute-start
Sparse Core Ops, SparseCore 0:
  11.4 203.2 all-gather.4
  234.7 35.8 all-gather.6
  734.4 59.6 reduce-scatter.2
where the time goes:
time: 806 us; the launch traced here: 804 us
  blocking collectives  356 us (44%)
  waiting for transfers between devices  219 us (27%)
  other arithmetic  75.1 us (9%)
  matrix products  69.3 us (9%)
  local copies, waits for them, and re-layouts  67.7 us (8%)
  between operations  15.2 us (2%)
    unnamed x1, blocking collectives  356 us
    all_gather x1, waiting for transfers between devices, on_device(): full_sections = lax.all_gather(projections[0], 'img', axis=3, tiled=True)  125 us
    reduce_scatter x1, waiting for transfers between devices, on_device(): lax.psum_scatter(spread.astype(jnp.bfloat16), 'cls', scatter_dimension=0,...  58.8 us
    dot_general x8, matrix products, back_class(): lax.dot_general(class_weights, flat_images, (((0,), (0,)), ((), ())), pre...  48.9 us
    convert_element_type x2, other arithmetic, on_device(): (ctf_rows[:, None, :] * images[0].astype(jnp.float32)).astype(jnp.bfloat16)  36.9 us
    all_gather x1, waiting for transfers between devices, on_device(): piece = lax.all_gather(full_sections, 'cls', axis=0, tiled=True)  34.9 us
    convert_element_type x1, local copies, waits for them, and re-layouts, on_device(): images[0].astype(jnp.float32)  24.2 us
    all_gather x1, local copies, waits for them, and re-layouts, on_device(): full_sections = lax.all_gather(projections[0], 'img', axis=3, tiled=True)  19.8 us
  transfers between devices with their start and end apart: 4, of which 3 were waited for; matrix products, arithmetic and copies ran while one was open for 10% of the time, Pallas kernels for 0%

commit v1 on v0

--- a/solution.py
+++ b/solution.py
@@ -81,7 +81,9 @@
     ctf_power = table * table * inverse
     translations = trans_ids[0]
     cosine, sine = phases(translations, freqs)
-    full_sections = lax.all_gather(projections[0], "img", axis=3, tiled=True)
+    full_sections = jnp.concatenate(
+        lax.all_to_all(jnp.stack([projections[0]] * lax.axis_size("img"), 0), "img", 0, 0), 3
+    )
     piece = lax.all_gather(full_sections, "cls", axis=0, tiled=True)
     number = piece.shape[0]
     shifted = shift_sections(piece, inverse, cosine, sine).reshape(number * O * TR, 2 * freqs)

time: 806 us -> 685 us (0.85)
  waiting for transfers between devices: 219 us -> 97.8 us
  starting transfers between devices: 1.33 us -> 16.4 us
  local copies, waits for them, and re-layouts: 67.7 us -> 55.3 us
    all_gather x1 -> x0, waiting for transfers between devices: 125 us -> none  [on_device(): full_sections = lax.all_gather(projections[0], 'img', axis=3, tiled=True)]
    all_gather x1 -> x0, local copies, waits for them, and re-layouts: 19.8 us -> none  [on_device(): full_sections = lax.all_gather(projections[0], 'img', axis=3, tiled=True)]
    all_to_all x0 -> x1, starting transfers between devices: none -> 15.1 us  [on_device(): lax.all_to_all(jnp.stack([projections[0]] * lax.axis_size('img'), 0), 'im...]
  transfers between devices with their start and end apart: 4 -> 4, of which waited for: 3 -> 2; matrix products, arithmetic and copies ran while one was open for 10% -> 12% of each run, Pallas kernels for 0% -> 0%
where the time goes in v1:
time: 685 us; the launch traced here: 683 us
  blocking collectives  356 us (52%)
  waiting for transfers between devices  97.8 us (14%)
  other arithmetic  72.1 us (11%)
  matrix products  69.7 us (10%)
  local copies, waits for them, and re-layouts  55.3 us (8%)
  starting transfers between devices  16.4 us (2%)
  between operations  15.6 us (2%)
    unnamed x1, blocking collectives  356 us
    reduce_scatter x1, waiting for transfers between devices, on_device(): lax.psum_scatter(spread.astype(jnp.bfloat16), 'cls', scatter_dimension=0,...  58.8 us
    dot_general x8, matrix products, back_class(): lax.dot_general(class_weights, flat_images, (((0,), (0,)), ((), ())), pre...  48.9 us
    all_gather x1, waiting for transfers between devices, on_device(): piece = lax.all_gather(full_sections, 'cls', axis=0, tiled=True)  38.9 us
    convert_element_type x2, other arithmetic, on_device(): (ctf_rows[:, None, :] * images[0].astype(jnp.float32)).astype(jnp.bfloat16)  36.7 us
    convert_element_type x1, local copies, waits for them, and re-layouts, on_device(): images[0].astype(jnp.float32)  24.2 us
    all_to_all x1, starting transfers between devices, on_device(): lax.all_to_all(jnp.stack([projections[0]] * lax.axis_size('img'), 0), 'im...  15.1 us
  transfers between devices with their start and end apart: 4, of which 2 were waited for; matrix products, arithmetic and copies ran while one was open for 12% of the time, Pallas kernels for 0%

profile of v1, /device:TPU:1, one launch (start us, length us, event | category | flops | bytes accessed | tf_op | source)
XLA Modules:
  0.0 683.4 jit_solution(7758079763381279656)
XLA Ops:
  8.1 1.6 stack.18
  9.7 15.1 %all-to-all-start = ((bf16[64,4,8,2,130]{4,2,1,3,0:T(8,128)(2,1)}), bf16[64,4,8,2,130]{4,2,1,3,0:T(8,128)(2,1)S(1)}, u32[]{:S(2)}, u32[]{:S(2)}) async-start(bf16[64,4,8,2,130]{4,2,1,3,0:T(8,128)(2,1)} %stack.18), calls=%async_computation | async-start | bytes 4194304 | tf_op jit(solution)/shard_map/all_to_all | solution.py:85
  25.6 5.7 fusion.25
  31.4 9.1 %copy.77 = f32[256,8320]{0,1:T(8,128)} copy(f32[256,8320]{1,0:T(8,128)} %fusion.25) | data formatting | bytes 17039360
  40.5 24.2 %copy.62 = f32[1,256,2,8320]{1,3,2,0:T(8,128)} copy(bf16[1,256,2,8320]{3,2,1,0:T(2,128)(2,1)} %param.10) | data formatting | bytes 25559040 | tf_op jit(solution)/shard_map/convert_element_type | solution.py:79
  64.7 25.2 %fusion.14 = bf16[256,16640]{0,1:T(8,128)(2,1)} fusion(f32[1,256,2,8320]{1,3,2,0:T(8,128)} %copy.62, f32[256,8320]{0,1:T(8,128)} %copy.77), kind=kLoop, calls=%fused_computation.20 | loop fusion | flops 8519680 | bytes 34078720 | tf_op jit(solution)/shard_map/convert_element_type | solution.py:79
  91.2 11.5 %fusion.16 = bf16[256,2,8320,1,1]{2,1,0,4,3:T(2,128)(2,1)} fusion(f32[256,8320]{1,0:T(8,128)} %fusion.25, bf16[1,256,2,8320]{3,2,1,0:T(2,128)(2,1)} %param.10), kind=kLoop, calls=%fused_computation.25 | loop fusion | flops 12779520 | bytes 25559040 | tf_op jit(solution)/shard_map/convert_element_type | solution.py:79
  102.7 2.5 copy.59
  105.2 4.4 reshape.297
  110.8 38.9 %all-gather.2.cloned.1.call-done = bf16[8,8,2,8320]{3,1,2,0:T(8,128)(2,1)} async-done(((bf16[4,8,2,8320]{3,1,2,0:T(8,128)(2,1)}), bf16[8,8,2,8320]{3,1,2,0:T(8,128)(2,1)}) %all-gather.2.cloned.1.call-update) | async-done | bytes 2129936 | tf_op jit(solution)/shard_map/all_gather | solution.py:87
  149.7 3.9 fusion.21
  154.3 7.7 %subtract_convert_fusion = (bf16[8,8,8,1,8320]{4,2,3,1,0:T(8,128)(2,1)}, bf16[8,8,8,1,8320]{4,2,3,1,0:T(8,128)(2,1)}) fusion(f32[8,8320]{1,0:T(8,128)S(1)} %get-tuple-element.141, f32[8,8,8320]{2,1,0:T(8,128)S(1)} %get-tuple-element.139, f32[8,8320]{1,0:T(8,128)S(1)} %get-tuple-element.140, f32[8,8,8320]{2,1,0:T(8,128)S(1)} %get-tuple-element.138), kind=kLoop, calls=%fused_computation.24 | loop fusion | flops 34078720 | bytes 21831680 | tf_op jit(solution)/shard_map/convert.2
  161.9 10.9 %select_reduce_fusion = (f32[256]{0:T(256)S(1)}, f32[256,8,8,8,1]{0,3,4,2,1:T(8,128)S(1)}) fusion(f32[256,8,8]{0,2,1:T(8,128)S(1)} %bitcast.144, pred[256,8]{0,1:T(8,128)(4,1)S(1)} %fusion.54, bf16[8,8,8,1,8320]{4,2,3,1,0:T(8,128)(2,1)} %get-tuple-element.137, bf16[8,8,8,1,8320]{4,2,3,1,0:T(8,128)(2,1)} %get-tuple-element.136, ...), kind=kOutput, calls=%fused_computation.54 | convolution fusion | flops 4396548096 | bytes 26151936 | tf_op jit(solution)/shard_map/dot_general | solution.py:52
  173.1 83.4 %while.12 = (s32[]{:T(128)}, f32[8,8,2,8320]{3,1,2,0:T(8,128)}, bf16[8,256,64]{1,2,0:T(8,128)(2,1)S(1)}, bf16[256,16640]{0,1:T(8,128)(2,1)}, f32[8320]{0:T(1024)...) while((s32[]{:T(128)}, f32[8,8,2,8320]{3,1,2,0:T(8,128)}, ...), condition=%wide.region_6.7_spmd.clone.clone, body=%wide.region_3.6_spmd.clone.clone.sunk | while | flops 549785600 | bytes 21931680 | solution.py:121
  174.2 6.1 fusion.68
  184.6 6.1 fusion.68
  195.0 6.1 fusion.68
  205.4 6.1 fusion.68
  215.9 6.1 fusion.68
  226.3 6.1 fusion.68
  236.7 6.1 fusion.68
  247.1 6.1 fusion.68
  256.5 356.2 %all-reduce.2 = bf16[8,8,2,8320]{3,1,2,0:T(8,128)(2,1)S(1)} all-reduce(f32[8,8,2,8320]{3,1,2,0:T(8,128)} %get-tuple-element.35), channel_id=2, replica_groups=mesh['half'=2,'cls'=2,'img'=64] {'img'}, use_global_device_ids=true, to_apply=%region_7.8.clone | all-reduce | flops 1064960 | bytes 6389760
  614.4 58.8 %reduce-scatter.3.cloned.1.call-done = bf16[4,8,2,130]{3,1,2,0:T(8,128)(2,1)} async-done(((bf16[8,8,2,130]{3,1,2,0:T(8,128)(2,1)}), bf16[4,8,2,130]{3,1,2,0:T(8,128)(2,1)}) %reduce-scatter.3.cloned.1.call-update) | async-done | bytes 16656 | tf_op jit(solution)/shard_map/reduce_scatter | solution.py:123
  (89 shorter events, 42.8 us)
Async XLA Ops:
  7.2 17.7 %copy-start.5 = (s32[1,8]{1,0:T(1,128)S(1)}, s32[1,8]{1,0:T(1,128)}, u32[]{:S(2)}) copy-start(s32[1,8]{1,0:T(1,128)} %param.15) | copy-start | bytes 100
  7.2 17.8 %copy-start.4 = (s32[1,256,4]{1,2,0:T(4,128)S(1)}, s32[1,256,4]{1,2,0:T(4,128)}, u32[]{:S(2)}) copy-start(s32[1,256,4]{1,2,0:T(4,128)} %param.14) | copy-start | bytes 12292
  7.2 18.4 %copy-start.1 = (f32[1,32,8320]{2,1,0:T(8,128)S(1)}, f32[1,32,8320]{2,1,0:T(8,128)}, u32[]{:S(2)}) copy-start(f32[1,32,8320]{2,1,0:T(8,128)} %param.12) | copy-start | bytes 3194884
  7.2 18.4 %copy-start.3 = (s32[1,256]{1,0:T(1,128)S(1)}, s32[1,256]{1,0:T(1,128)}, u32[]{:S(2)}) copy-start(s32[1,256]{1,0:T(1,128)} %param.13) | copy-start | bytes 3076
  9.7 93.0 %all-to-all-start = ((bf16[64,4,8,2,130]{4,2,1,3,0:T(8,128)(2,1)}), bf16[64,4,8,2,130]{4,2,1,3,0:T(8,128)(2,1)S(1)}, u32[]{:S(2)}, u32[]{:S(2)}) async-start(bf16[64,4,8,2,130]{4,2,1,3,0:T(8,128)(2,1)} %stack.18), calls=%async_computation | async-start | bytes 4194304 | tf_op jit(solution)/shard_map/all_to_all | solution.py:85
  24.8 124.9 %all-gather.2.cloned.1.call-start = ((), (), s32[]{:S(2)}) async-start(), calls=%async_computation.2 | async-start | bytes 3194880 | tf_op jit(solution)/shard_map/all_gather | solution.py:87
  40.5 24.2 %copy-start.2 = (f32[1,8320]{1,0:T(1,128)S(1)}, f32[1,8320]{1,0:T(1,128)}, u32[]{:S(2)}) copy-start(f32[1,8320]{1,0:T(1,128)} %param.16) | copy-start | bytes 99844
  64.7 25.2 %copy-start.6 = (u32[256]{0:T(256)S(1)}, u32[256]{0:T(256)}, u32[]{:S(2)}) copy-start(u32[256]{0:T(256)} %constant.79) | copy-start | bytes 3076
  109.7 563.5 %reduce-scatter.3.cloned.1.call-start = ((), (), s32[]{:S(2)}) async-start(), calls=%async_computation.3 | async-start | bytes 98304 | tf_op jit(solution)/shard_map/reduce_scatter | solution.py:123
  149.7 4.3 copy-start
  673.2 2.6 collective-permute-start
Sparse Core Ops, SparseCore 0:
  109.8 39.8 all-gather.1
  613.6 59.6 reduce-scatter.2
